TPU v7x, 128 devices: a whole 4x4x4 slice. The times are simulated.
128 devices in a mesh: gz: 4 (over z_hi, core), gy: 32 (over y, z_lo, x).
Axes of the slice: x: 4, y: 4, z: 4 (z_hi: 2, z_lo: 2; z = z_hi * 2 + z_lo), core: 2. Of those that a mesh axis runs over, the one named last changes fastest.
Arguments:
- velocity: float32 [3, 256, 256, 512], P(None, None, 'gy', 'gz'), may hold values from -0.3 to 0.3
- increment: float32 [3, 256, 256, 512], P(None, None, 'gy', 'gz'), may hold values from -4 to 4
- template: bfloat16 [256, 256, 512], P(None, 'gy', 'gz'), may hold values from 0 to 1
- deformed: bfloat16 [256, 256, 512], P(None, 'gy', 'gz'), may hold values from 0 to 1
Outputs:
- preconditioned: float32 [3, 256, 256, 512], P(None, None, 'gy', 'gz')
All inputs are finite; a program needn't handle non-finite values.
Results may differ from a plain program's by a relative error of at most 0.0003.
Values sent between devices are 32-bit elements; how exact they have to be, the bound alone decides.
A program may use at most 256 MiB of HBM per device.

v0:
```python
import functools
import math

import jax
import jax.numpy as jnp
import numpy as np
from jax import lax
from jax.experimental import pallas as pl
from jax.experimental.pallas import tpu as pltpu
from jax.sharding import PartitionSpec as P

MESH = pl.DeviceIdType.MESH
BETA = 0.02
GAMMA = 0.05
COARSE_BETA = 0.025
OMEGA = 1.0 / (0.05 + 42.0 * 0.02)

NX = 256
NR = NX * 8
GY = 32
GZ = 4
CX, CY, CZ = 64, 64, 128
PACK = 32
GROUP = 4
NG = NX // GROUP
HIGH = lax.Precision.HIGHEST


def cas(rows, cols, count):
    angle = (np.outer(rows, cols) % count) * (2.0 * math.pi / count)
    return (np.cos(angle) + np.sin(angle)).astype(np.float32)


def eigen(count):
    return 2.0 - 2.0 * np.cos(np.arange(count) * (2.0 * math.pi / count))


def tables():
    owned = np.concatenate([2 * np.arange(GY), 2 * np.arange(GY) + 1])
    all_x, all_y, all_z = np.arange(CX), np.arange(CY), np.arange(CZ)
    forward_x = cas(owned, all_x, CX)
    inverse_x = cas(all_x, owned, CX)
    forward_y = np.concatenate([cas(all_y, (2 * np.arange(GY) - 1 + j) % CY, CY) for j in range(4)])
    inverse_y = cas(np.concatenate([2 * np.arange(GY), 2 * np.arange(GY) + 1]), all_y, CY)
    both_z = cas(all_z, all_z, CZ)
    gather_z = np.zeros((4 * 128, 128), np.float32)
    spread_z = np.zeros((128, 4 * 128), np.float32)
    for j in range(4):
        for z in range(128):
            gather_z[j * 128 + z, j * 32 + z // 4] = 1.0 / 64.0
            spread_z[j * 32 + z // 4, j * 128 + z] = 1.0
    eigen_yz = (eigen(CY)[:, None] + eigen(CZ)[None, :]).astype(np.float32)
    eigen_x = np.repeat(eigen(CX)[:, None], 128, axis=1).astype(np.float32)
    return (forward_x, inverse_x, forward_y, inverse_y, both_z, gather_z, spread_z, eigen_yz, eigen_x)


def mm(a, b):
    return jnp.dot(a, b, precision=HIGH, preferred_element_type=jnp.float32)


def first(x):
    return pl.multiple_of(x, 8)


def action(
    v_hbm, u_hbm, t_hbm, d_hbm,
    fx, ix, fy, iy, bz, gz_tab, sz, eyz, ex,
    h_hbm, rim_hbm, k_out,
    vel, inc, tb, db, tf, df, s1, a2, w, hs, g0y, g0z, g1y, g1z,
    zsend, zfrom, zpad, wpad, ssend, sfrom, spad, qsend, qfrom, qpad,
    tysend, tyfrom, sysend, syfrom, qysend, qyfrom, rims,
    su, sw, sh, fsend, frecv, bsend, brecv,
    load_sem, zs, zr, ys, yr, rs, rr, fs, fr, bs, br, store_sem,
):
    gz = lax.axis_index("gz")
    gy = lax.axis_index("gy")
    ynext, yprev = lax.rem(gy + 1, GY), lax.rem(gy + GY - 1, GY)
    znext, zprev = lax.rem(gz + 1, GZ), lax.rem(gz + GZ - 1, GZ)
    row = lax.broadcasted_iota(jnp.int32, (8, 128), 0)
    lane = lax.broadcasted_iota(jnp.int32, (8, 128), 1)
    slot = lax.rem(lax.shift_right_logical(lane + 2, 2), PACK)
    low_half = lax.rem(lane + 2, 4) < 2

    barrier = pltpu.get_barrier_semaphore()

    def peer(k):
        return (lax.rem(gz + k // GY, GZ), lax.rem(gy + lax.rem(k, GY), GY))

    def greet(k, carry):
        pl.semaphore_signal(barrier, inc=1, device_id=peer(k), device_id_type=MESH)
        return carry

    loads = [
        pltpu.make_async_copy(src, dst, load_sem.at[i])
        for i, (src, dst) in enumerate(
            [(t_hbm, tb), (d_hbm, db)]
            + [(u_hbm.at[pl.ds(c * NR, NR)], inc.at[pl.ds(c * NR, NR)]) for c in range(3)]
            + [(v_hbm.at[pl.ds(c * NR, NR)], vel.at[pl.ds(c * NR, NR)]) for c in range(3)]
        )
    ]
    for load in loads:
        load.start()
    lax.fori_loop(1, GY * GZ, greet, 0)

    def plane(ref, c, x):
        return ref[pl.ds(first(c * NR + x * 8), 8), :]

    def window(ref, c, i):
        at = [lax.rem(GROUP * i + NX - 1, NX)] + [GROUP * i + q for q in range(GROUP)]
        at.append(lax.rem(GROUP * i + GROUP, NX))
        return [plane(ref, c, x) for x in at]

    def roll(value, shift, axis):
        return pltpu.roll(value, shift % value.shape[axis], axis)

    def pack_into(acc, value, p):
        return jnp.where(slot == p, pltpu.roll(value, 4 * p, 1), acc)

    def unpacked(ref, f, i, q):
        tile = ref[pl.ds(first(f * 64 + (i // 8) * 8), 8), :]
        p = GROUP * lax.rem(i, 8) + q
        return pltpu.roll(tile, lax.rem(128 - 4 * p, 128), 1)

    def z_sides(value, outer):
        up = roll(jnp.where(lane == 0, outer, value), -1, 1)
        down = roll(jnp.where(lane == 127, outer, value), 1, 1)
        return up, down

    def y_sides(value, above, below):
        up = jnp.where(row == 7, above, roll(value, -1, 0))
        down = jnp.where(row == 0, below, roll(value, 1, 0))
        return up, down

    def halo_row(ref, k, x):
        return jnp.broadcast_to(ref[pl.ds(k * NX + x, 1), :], (8, 128))

    def spread(ref, base, k, r):
        return ref[pl.ds(base + 64 * k + r, 8, stride=8), :]

    def z_pair(send, got, sems, base, sem_at):
        size = send.shape[0]
        return [
            pltpu.make_async_remote_copy(
                src_ref=send, dst_ref=got.at[side], send_sem=sems[0].at[sem_at + side],
                recv_sem=sems[1].at[sem_at + side], device_id=(to, gy), device_id_type=MESH)
            for side, to in ((0, znext), (1, zprev))
        ]

    def y_pair(send, got, sems, sem_at):
        return [
            pltpu.make_async_remote_copy(
                src_ref=send.at[side], dst_ref=got.at[side], send_sem=sems[0].at[sem_at + side],
                recv_sem=sems[1].at[sem_at + side], device_id=(gz, to), device_id_type=MESH)
            for side, to in ((0, ynext), (1, yprev))
        ]

    def combine(got, pad, count):
        def one(k, carry):
            at = pl.ds(first(k * 8), 8)
            pad[at, :] = jnp.where(low_half, got[0, at, :], got[1, at, :])
            return carry
        lax.fori_loop(0, count * 8, one, 0)

    loads[0].wait()
    loads[1].wait()

    def widen(k, carry):
        at = pl.ds(pl.multiple_of(k * 64, 64), 64)
        tf[at, :] = tb[at, :].astype(jnp.float32)
        df[at, :] = db[at, :].astype(jnp.float32)
        return carry

    lax.fori_loop(0, NR // 64, widen, 0)

    def state_rows(k, carry):
        at = pl.ds(first(8 * k), 8)
        also = pl.ds(first(NX + 8 * k), 8)
        tysend[0, at, :] = spread(tf, 0, k, 7)
        tysend[0, also, :] = spread(df, 0, k, 7)
        tysend[1, at, :] = spread(tf, 0, k, 0)
        tysend[1, also, :] = spread(df, 0, k, 0)
        return carry

    lax.fori_loop(0, NX // 8, state_rows, 0)
    for c in range(3):
        loads[2 + c].wait()
    sources = [(tf, 0), (df, 0), (inc, 0), (inc, 1), (inc, 2)]

    def pack_inputs(k, carry):
        def some(m, accs):
            for q in range(GROUP):
                p = GROUP * m + q
                accs = tuple(
                    pack_into(acc, plane(ref, c, PACK * k + p), p) for acc, (ref, c) in zip(accs, sources)
                )
            return accs
        accs = lax.fori_loop(0, PACK // GROUP, some, tuple(jnp.zeros((8, 128), jnp.float32) for _ in sources))
        for f, acc in enumerate(accs):
            zsend[pl.ds(first(f * 64 + k * 8), 8), :] = acc
        return carry

    lax.fori_loop(0, NX // PACK, pack_inputs, 0)
    pl.semaphore_wait(barrier, GY * GZ - 1)
    state_copies = y_pair(tysend, tyfrom, (ys, yr), 0)
    edge_copies = z_pair(zsend, zfrom, (zs, zr), 0, 0)
    for copy in edge_copies + state_copies:
        copy.start()

    for copy in edge_copies:
        copy.wait_recv()
    combine(zfrom, zpad, 5)

    def edge_laplacian(n, carry):
        c, k = n // 8, lax.rem(n, 8)
        base = 128 + c * 64

        def tile(ref, m):
            return ref[pl.ds(first(base + m * 8), 8), :]

        here, own = tile(zpad, k), tile(zsend, k)
        before, after = tile(zpad, lax.rem(k + 7, 8)), tile(zpad, lax.rem(k + 1, 8))
        x_down = jnp.where(slot == 0, roll(before, 4, 1), roll(here, 4, 1))
        x_up = jnp.where(slot == PACK - 1, roll(after, -4, 1), roll(here, -4, 1))
        y_up, y_down = y_sides(here, 0.0, 0.0)
        z_sum = jnp.where(low_half, roll(here, 1, 1) + roll(own, -1, 1), roll(here, -1, 1) + roll(own, 1, 1))
        wpad[pl.ds(first(c * 64 + k * 8), 8), :] = 6.0 * here - (x_down + x_up) - (y_up + y_down) - z_sum
        return carry

    lax.fori_loop(0, 24, edge_laplacian, 0)

    def laplacian(i, carry):
        for c in range(3):
            cells = window(inc, c, i)
            sum_u = jnp.zeros((8, 128), jnp.float32)
            sum_w = jnp.zeros((8, 128), jnp.float32)
            for q in range(GROUP):
                u = cells[q + 1]
                z_up, z_down = z_sides(u, unpacked(zpad, 2 + c, i, q))
                y_up, y_down = y_sides(u, 0.0, 0.0)
                lap = 6.0 * u - (cells[q] + cells[q + 2]) - (y_up + y_down) - (z_up + z_down)
                w[pl.ds(first(c * NR + (GROUP * i + q) * 8), 8), :] = lap
                sum_u = sum_u + u
                sum_w = sum_w + lap
            su[pl.ds(first(c * 512 + i * 8), 8), :] = sum_u
            sw[pl.ds(first(c * 512 + i * 8), 8), :] = sum_w
        return carry

    lax.fori_loop(0, NG, laplacian, 0)

    def rim_rows(n, carry):
        c, k = n // 32, lax.rem(n, 32)
        base = c * NR
        at = pl.ds(first(8 * k), 8)
        scale = OMEGA * BETA
        last, first_row = spread(inc, base, k, 7), spread(inc, base, k, 0)
        rims[0, c, 0, at, :] = -scale * (spread(inc, base, k, 6) + 2.0 * spread(w, base, k, 7))
        rims[0, c, 1, at, :] = scale * last
        rims[1, c, 0, at, :] = -scale * (spread(inc, base, k, 1) + 2.0 * spread(w, base, k, 0))
        rims[1, c, 1, at, :] = scale * first_row
        return carry

    lax.fori_loop(0, 96, rim_rows, 0)
    rim_copies = [
        [
            pltpu.make_async_remote_copy(
                src_ref=rims.at[side, c], dst_ref=rim_hbm.at[side, c], send_sem=rs.at[side * 3 + c],
                recv_sem=rr.at[side * 3 + c], device_id=(gz, to), device_id_type=MESH)
            for side, to in ((0, ynext), (1, yprev))
        ]
        for c in range(3)
    ]

    for copy in state_copies:
        copy.wait_recv()

    def differences(ref, field, i, keep_y, keep_z):
        cells = window(ref, 0, i)
        out = []
        for q in range(GROUP):
            x = GROUP * i + q
            z_up, z_down = z_sides(cells[q + 1], unpacked(zpad, field, i, q))
            y_up, y_down = y_sides(
                cells[q + 1], halo_row(tyfrom.at[1], field, x), halo_row(tyfrom.at[0], field, x))
            dy, dz = y_up - y_down, z_up - z_down
            keep_y[pl.ds(first(x * 8), 8), :] = dy
            keep_z[pl.ds(first(x * 8), 8), :] = dz
            out.append((cells[q + 2] - cells[q], dy, dz))
        return out

    def first_state(k, carry):
        def some(m, acc):
            i = 8 * k + m
            for q, (dx, dy, dz) in enumerate(differences(tf, 0, i, g0y, g0z)):
                x = GROUP * i + q
                value = -0.25 * (plane(inc, 0, x) * dx + plane(inc, 1, x) * dy + plane(inc, 2, x) * dz)
                s1[pl.ds(first(x * 8), 8), :] = value
                acc = pack_into(acc, value, GROUP * m + q)
            return acc
        ssend[pl.ds(first(k * 8), 8), :] = lax.fori_loop(0, PACK // GROUP, some, jnp.zeros((8, 128), jnp.float32))
        return carry

    lax.fori_loop(0, NX // PACK, first_state, 0)

    def s1_rows(k, carry):
        at = pl.ds(first(8 * k), 8)
        sysend[0, at, :] = spread(s1, 0, k, 7)
        sysend[1, at, :] = spread(s1, 0, k, 0)
        return carry

    lax.fori_loop(0, NX // 8, s1_rows, 0)
    s1_copies = z_pair(ssend, sfrom, (zs, zr), 0, 2) + y_pair(sysend, syfrom, (ys, yr), 2)
    for copy in s1_copies:
        copy.start()
    for copy in rim_copies[0]:
        copy.start()

    def fine(i, carry):
        for c in range(3):
            cells = window(w, c, i)
            for q in range(GROUP):
                x = GROUP * i + q
                u, lap = plane(inc, c, x), cells[q + 1]
                z_up, z_down = z_sides(lap, unpacked(wpad, c, i, q))
                y_up, y_down = y_sides(lap, -u, -u)
                twice = 6.0 * lap - (cells[q] + cells[q + 2]) - (y_up + y_down) - (z_up + z_down)
                hs[pl.ds(first(c * NR + x * 8), 8), :] = (OMEGA * GAMMA) * u + (OMEGA * BETA) * twice
        return carry

    lax.fori_loop(0, NG, fine, 0)

    for c in range(3):
        loads[5 + c].wait()
    for copy in s1_copies:
        copy.wait_recv()
    combine(sfrom, spad, 1)

    def second_state(k, carry):
        def some(m, acc):
            i = 8 * k + m
            cells = window(s1, 0, i)
            for q, (dx, dy, dz) in enumerate(differences(df, 1, i, g1y, g1z)):
                x = GROUP * i + q
                s = cells[q + 1]
                z_up, z_down = z_sides(s, unpacked(spad, 0, i, q))
                y_up, y_down = y_sides(s, halo_row(syfrom.at[1], 0, x), halo_row(syfrom.at[0], 0, x))
                moved = 0.5 * (plane(inc, 0, x) * dx + plane(inc, 1, x) * dy + plane(inc, 2, x) * dz)
                speed_z = None
                for c, (up, down) in enumerate(((cells[q + 2], cells[q]), (y_up, y_down), (z_up, z_down))):
                    speed = plane(vel, c, x)
                    moved = moved + jnp.maximum(speed, 0.0) * (s - down) + jnp.minimum(speed, 0.0) * (up - s)
                    speed_z = speed
                value = 0.5 * moved - s
                a2[pl.ds(first(x * 8), 8), :] = value
                sent = jnp.where(lane >= 64, jnp.minimum(speed_z, 0.0), jnp.maximum(speed_z, 0.0)) * value
                acc = pack_into(acc, sent, GROUP * m + q)
            return acc
        qsend[pl.ds(first(k * 8), 8), :] = lax.fori_loop(0, PACK // GROUP, some, jnp.zeros((8, 128), jnp.float32))
        return carry

    lax.fori_loop(0, NX // PACK, second_state, 0)

    def flux_rows(k, carry):
        at = pl.ds(first(8 * k), 8)
        qysend[0, at, :] = jnp.minimum(spread(vel, NR, k, 7), 0.0) * spread(a2, 0, k, 7)
        qysend[1, at, :] = jnp.maximum(spread(vel, NR, k, 0), 0.0) * spread(a2, 0, k, 0)
        return carry

    lax.fori_loop(0, NX // 8, flux_rows, 0)
    flux_copies = z_pair(qsend, qfrom, (zs, zr), 0, 4) + y_pair(qysend, qyfrom, (ys, yr), 4)
    for copy in flux_copies:
        copy.start()
    for copy in rim_copies[1]:
        copy.start()
    for copy in flux_copies:
        copy.wait_recv()
    combine(qfrom, qpad, 1)

    def adjoint(i, carry):
        cells_a = window(a2, 0, i)
        cells_v = window(vel, 0, i)
        cells_t = window(tf, 0, i)
        cells_d = window(df, 0, i)
        sums = [jnp.zeros((8, 128), jnp.float32) for _ in range(3)]
        for q in range(GROUP):
            x = GROUP * i + q
            a = cells_a[q + 1]
            vy, vz = plane(vel, 1, x), plane(vel, 2, x)
            size = jnp.abs(cells_v[q + 1]) + jnp.abs(vy) + jnp.abs(vz)
            change = jnp.maximum(cells_v[q + 2], 0.0) * cells_a[q + 2]
            change = change - jnp.minimum(cells_v[q], 0.0) * cells_a[q] - size * a
            qy, py = jnp.minimum(vy, 0.0) * a, jnp.maximum(vy, 0.0) * a
            change = change + jnp.where(row == 7, halo_row(qyfrom.at[1], 0, x), roll(py, -1, 0))
            change = change - jnp.where(row == 0, halo_row(qyfrom.at[0], 0, x), roll(qy, 1, 0))
            qz, pz = jnp.minimum(vz, 0.0) * a, jnp.maximum(vz, 0.0) * a
            outer = unpacked(qpad, 0, i, q)
            change = change + roll(jnp.where(lane == 0, outer, pz), -1, 1)
            change = change - roll(jnp.where(lane == 127, outer, qz), 1, 1)
            scaled = (0.25 * OMEGA) * (a + 0.5 * change)
            other = (0.25 * OMEGA) * a
            pairs = (
                (cells_t[q + 2] - cells_t[q], cells_d[q + 2] - cells_d[q]),
                (plane(g0y, 0, x), plane(g1y, 0, x)),
                (plane(g0z, 0, x), plane(g1z, 0, x)),
            )
            for c, (from_t, from_d) in enumerate(pairs):
                value = plane(hs, c, x) + scaled * from_t + other * from_d
                hs[pl.ds(first(c * NR + x * 8), 8), :] = value
                sums[c] = sums[c] + value
        for c in range(3):
            sh[pl.ds(first(c * 512 + i * 8), 8), :] = sums[c]
        return carry

    lax.fori_loop(0, NG, adjoint, 0)
    store = pltpu.make_async_copy(hs, h_hbm, store_sem)
    store.start()

    def rows_of(ref, c, r):
        return ref[pl.ds(c * 512 + r, CX, stride=8), :]

    parts = []
    for c in range(3):
        scale = OMEGA * BETA
        parts.append(scale * (rows_of(su, c, 0) - rows_of(su, c, 1) - 2.0 * rows_of(sw, c, 0)))
        for half in (0, 4):
            parts.append(
                (rows_of(sh, c, half) + rows_of(sh, c, half + 1))
                + (rows_of(sh, c, half + 2) + rows_of(sh, c, half + 3)))
        parts.append(scale * (rows_of(su, c, 7) - rows_of(su, c, 6) - 2.0 * rows_of(sw, c, 7)))
    for c in range(3):
        lines = mm(fx[...], jnp.concatenate(parts[4 * c:4 * c + 4], axis=1))
        lines = mm(lines, gz_tab[...])
        for h in range(2):
            block = lines[h * GY:(h + 1) * GY]
            if c < 2:
                fsend[h, :, c, :] = block
            else:
                fsend[2 + h, :, 0, :] = block
                fsend[2 + h, :, 1, :] = block

    def exchange(send, got, ssems, rsem):
        def copy_to(k):
            z, y = peer(k)
            return pltpu.make_async_remote_copy(
                src_ref=send.at[z, y], dst_ref=got.at[gz, gy], send_sem=ssems.at[k], recv_sem=rsem,
                device_id=(z, y), device_id_type=MESH)

        def begin(k, carry):
            copy_to(k).start()
            return carry

        def drain(k, carry):
            copy_to(k).wait_send()
            return carry

        lax.fori_loop(1, GY * GZ, begin, 0)
        pltpu.make_async_copy(send.at[gz, gy], got.at[gz, gy], rsem).start()

        def finish():
            pltpu.make_async_copy(got, got, rsem).wait()

        def done():
            lax.fori_loop(1, GY * GZ, drain, 0)

        return finish, done

    arrive, sent_forward = exchange(fsend, frecv, fs, fr)
    for copy in rim_copies[2]:
        copy.start()
    total = eyz[...] + ex[pl.ds(2 * gy + lax.rem(gz, 2), 1), :]
    factor = (1.0 / (GAMMA + COARSE_BETA * total * total) - OMEGA) * (1.0 / (OMEGA * CX * CY * CZ))
    arrive()
    lane64 = lax.broadcasted_iota(jnp.int32, (CY, 128), 1) // 32
    lane32 = lax.broadcasted_iota(jnp.int32, (GY, 128), 1) // 32
    solved = []
    for s in range(2):
        whole = jnp.zeros((CY, 128), jnp.float32)
        for zb in range(GZ):
            lines = mm(fy[...], frecv[zb, :, s, :])
            merged = jnp.zeros((CY, 128), jnp.float32)
            for j in range(4):
                moved = roll(lines[j * CY:(j + 1) * CY], 32 * (zb - j), 1)
                merged = merged + moved
            whole = jnp.where(lane64 == zb, merged, whole)
        modes = mm(whole, bz[...]) * factor
        solved.append(mm(iy[...], mm(modes, bz[...])))
    for zb in range(GZ):
        block = jnp.zeros((GY, 128), jnp.float32)
        for s in range(2):
            for half in range(2):
                part = roll(solved[s][half * GY:(half + 1) * GY], 32 * (2 * s + half - zb), 1)
                block = jnp.where(lane32 == 2 * s + half, part, block)
        bsend[zb, :, 0, :] = block
    arrive, sent_back = exchange(bsend, brecv, bs, br)
    sent_forward()
    arrive()
    for k in range(2):
        modes = jnp.concatenate([brecv[2 * k, :, 0, :], brecv[2 * k + 1, :, 0, :]], axis=0)
        lines = mm(ix[...], modes)
        count = 4 if k == 0 else 2
        wide = mm(lines, sz[:, :count * 128])
        for n in range(count):
            k_out[pl.ds((4 * k + n) * CX, CX), :] = wide[:, n * 128:(n + 1) * 128]

    sent_back()
    for copy in edge_copies + state_copies + s1_copies + flux_copies:
        copy.wait_send()
    for pair in rim_copies:
        for copy in pair:
            copy.wait()
    store.wait()


def finish(h_ref, rim_ref, k_ref, out_ref):
    row = lax.broadcasted_iota(jnp.int32, (8, 128), 0)
    planes = h_ref.shape[1]

    def one(n, carry):
        for q in range(4):
            p = 4 * n + q
            for c in range(3):
                def wide(ref):
                    return jnp.broadcast_to(ref[pl.ds(p, 1), :], (8, 128))

                def coarse(half):
                    return jnp.broadcast_to(k_ref[2 * c + half, pl.ds(n, 1), :], (8, 128))

                rim = jnp.where(row < 4, coarse(0), coarse(1))
                for at, side, kind in ((0, 0, 0), (1, 0, 1), (6, 1, 1), (7, 1, 0)):
                    rim = rim + jnp.where(row == at, wide(rim_ref.at[side, c, kind]), 0.0)
                out_ref[c, p] = h_ref[c, p] + rim
        return carry

    lax.fori_loop(0, planes // 4, one, 0)


def per_device(velocity, increment, template, deformed):
    consts = [jnp.asarray(t) for t in tables()]
    f32 = jnp.float32
    vm = lambda *shape: pltpu.VMEM(shape, f32)
    dma = pltpu.SemaphoreType.DMA
    hessian, rims, coarse = pl.pallas_call(
        action,
        out_shape=(
            jax.ShapeDtypeStruct((3 * NR, 128), f32),
            jax.ShapeDtypeStruct((2, 3, 2, NX, 128), f32),
            jax.ShapeDtypeStruct((6 * CX, 128), f32),
        ),
        in_specs=[pl.BlockSpec(memory_space=pl.ANY)] * 4 + [pl.BlockSpec(memory_space=pltpu.VMEM)] * len(consts),
        out_specs=(
            pl.BlockSpec(memory_space=pl.ANY),
            pl.BlockSpec(memory_space=pl.ANY),
            pl.BlockSpec(memory_space=pltpu.VMEM),
        ),
        scratch_shapes=[
            vm(3 * NR, 128), vm(3 * NR, 128),
            pltpu.VMEM((NR, 128), jnp.bfloat16), pltpu.VMEM((NR, 128), jnp.bfloat16),
            vm(NR, 128), vm(NR, 128), vm(NR, 128), vm(NR, 128), vm(3 * NR, 128), vm(3 * NR, 128),
            vm(NR, 128), vm(NR, 128), vm(NR, 128), vm(NR, 128),
            vm(320, 128), vm(2, 320, 128), vm(320, 128), vm(192, 128),
            vm(64, 128), vm(2, 64, 128), vm(64, 128), vm(64, 128), vm(2, 64, 128), vm(64, 128),
            vm(2, 2 * NX, 128), vm(2, 2 * NX, 128), vm(2, NX, 128), vm(2, NX, 128), vm(2, NX, 128), vm(2, NX, 128),
            vm(2, 3, 2, NX, 128),
            vm(3 * 512, 128), vm(3 * 512, 128), vm(3 * 512, 128),
            vm(GZ, GY, 2, 128), vm(GZ, GY, 2, 128), vm(GZ, GY, 1, 128), vm(GZ, GY, 1, 128),
            dma((8,)), dma((6,)), dma((6,)), dma((6,)), dma((6,)), dma((6,)), dma((6,)),
            dma((GY * GZ,)), dma, dma((GY * GZ,)), dma, dma,
        ],
        compiler_params=pltpu.CompilerParams(
            collective_id=1, has_side_effects=True, vmem_limit_bytes=56 * 1024 * 1024),
        name="action",
    )(
        velocity.reshape(3 * NR, 128), increment.reshape(3 * NR, 128),
        template.reshape(NR, 128), deformed.reshape(NR, 128), *consts,
    )
    step = 32
    return pl.pallas_call(
        finish,
        grid=(NX // step,),
        out_shape=jax.ShapeDtypeStruct((3, NX, 8, 128), f32),
        in_specs=[
            pl.BlockSpec((3, step, 8, 128), lambda i: (0, i, 0, 0)),
            pl.BlockSpec((2, 3, 2, step, 128), lambda i: (0, 0, 0, i, 0)),
            pl.BlockSpec((6, step // 4, 128), lambda i: (0, i, 0)),
        ],
        out_specs=pl.BlockSpec((3, step, 8, 128), lambda i: (0, i, 0, 0)),
        name="finish",
    )(hessian.reshape(3, NX, 8, 128), rims, coarse.reshape(6, CX, 128))


def solution(mesh):
    placed = (
        P(None, None, "gy", "gz"),
        P(None, None, "gy", "gz"),
        P(None, "gy", "gz"),
        P(None, "gy", "gz"),
    )
    return jax.shard_map(
        per_device, mesh=mesh, in_specs=placed, out_specs=P(None, None, "gy", "gz"), check_vma=False
    )
```

profile of v0, /device:TPU:1, one launch (start us, length us, event | category | flops | bytes accessed | tf_op | source)
XLA Modules:
  0.0 133.2 jit_solution(7155827481006369107)
XLA Ops:
  0.0 126.1 %action.1 = (f32[6144,128]{1,0:T(8,128)}, f32[2,3,2,256,128]{4,3,2,1,0:T(8,128)}, f32[384,128]{1,0:T(8,128)}) custom-call(f32[6144,128]{1,0:T(8,128)} %bitcast.6, f32[6144,128]{1,0:T(8,128)} %bitcast.7, bf16[2048,128]{1,0:T(8,128)(2,1)} %bitcast.9, bf16[2048,128]{1,0:T(8,128)(2,1)} %bitcast.10, f32[64,64]{1,0:T(8,128)} %constant.16.clone.fx.iy, ...), custom_call_target="tpu_custom_call" | custom-call | tf_op jit(solution)/shard_map/action/pallas_call | solution.py:541
  126.1 7.0 %finish.1 = f32[3,256,8,128]{3,2,1,0:T(8,128)} custom-call(f32[3,256,8,128]{3,2,1,0:T(8,128)} %bitcast.8, f32[2,3,2,256,128]{4,3,2,1,0:T(8,128)} %get-tuple-element.9.rim_ref, f32[6,64,128]{2,1,0:T(8,128)} %bitcast.11), custom_call_target="tpu_custom_call" | custom-call | tf_op jit(solution)/shard_map/finish/pallas_call | solution.py:576
where the time goes:
time: 133 us
  Pallas kernels  133 us (100%)
    pallas_call x1, Pallas kernels, per_device(): pl.pallas_call(action, out_shape=(jax.ShapeDtypeStruct((3 * NR, 128), f32...  126 us
    pallas_call x1, Pallas kernels, per_device(): pl.pallas_call(finish, grid=(NX // step,), out_shape=jax.ShapeDtypeStruct...  7.05 us

commit v1 on v0

v1 whole, which is shorter than its diff:
```python
import functools
import math

import jax
import jax.numpy as jnp
import numpy as np
from jax import lax
from jax.experimental import pallas as pl
from jax.experimental.pallas import tpu as pltpu
from jax.sharding import PartitionSpec as P

MESH = pl.DeviceIdType.MESH
BETA = 0.02
GAMMA = 0.05
COARSE_BETA = 0.025
OMEGA = 1.0 / (0.05 + 42.0 * 0.02)

NX = 256
NR = NX * 8
GY = 32
GZ = 4
CX, CY, CZ = 64, 64, 128
PACK = 32
GROUP = 4
PAD = 8


def cas(rows, cols, count):
    angle = (np.outer(rows, cols) % count) * (2.0 * math.pi / count)
    return (np.cos(angle) + np.sin(angle)).astype(np.float32)


def eigen(count):
    return 2.0 - 2.0 * np.cos(np.arange(count) * (2.0 * math.pi / count))


def tables():
    owned = np.concatenate([2 * np.arange(GY), 2 * np.arange(GY) + 1])
    all_x, all_y, all_z = np.arange(CX), np.arange(CY), np.arange(CZ)
    forward_x = cas(owned, all_x, CX)
    inverse_x = cas(all_x, owned, CX)
    forward_y = np.concatenate([cas(all_y, (2 * np.arange(GY) - 1 + j) % CY, CY) for j in range(4)])
    inverse_y = cas(np.concatenate([2 * np.arange(GY), 2 * np.arange(GY) + 1]), all_y, CY)
    both_z = cas(all_z, all_z, CZ)
    gather_z = np.zeros((4 * 128, 128), np.float32)
    spread_z = np.zeros((128, 4 * 128), np.float32)
    for j in range(4):
        for z in range(128):
            gather_z[j * 128 + z, j * 32 + z // 4] = 1.0 / 64.0
            spread_z[j * 32 + z // 4, j * 128 + z] = 1.0
    eigen_yz = (eigen(CY)[:, None] + eigen(CZ)[None, :]).astype(np.float32)
    eigen_x = np.repeat(eigen(CX)[:, None], 128, axis=1).astype(np.float32)
    pairs = []
    for table in (forward_x, inverse_x, forward_y, inverse_y, both_z):
        high = table.astype(jnp.bfloat16)
        pairs += [high, (table - high.astype(np.float32)).astype(jnp.bfloat16)]
    return (*pairs, gather_z.astype(jnp.bfloat16), spread_z.astype(jnp.bfloat16), eigen_yz, eigen_x)


TABLES = 14


def halves(value):
    high = value.astype(jnp.bfloat16)
    return high, (value - high.astype(jnp.float32)).astype(jnp.bfloat16)


def mm(a, b):
    (ah, al), (bh, bl) = (x if isinstance(x, tuple) else halves(x) for x in (a, b))
    total = jnp.dot(ah, bh, preferred_element_type=jnp.float32)
    for x, y in ((ah, bl), (al, bh)):
        if x is not None and y is not None:
            total = total + jnp.dot(x, y, preferred_element_type=jnp.float32)
    return total


def first(x):
    return pl.multiple_of(x, 8)


def action(
    v_hbm, u_hbm, t_hbm, d_hbm,
    *refs,
):
    tables_hbm, refs = refs[:TABLES], refs[TABLES:]
    (h_hbm, rim_hbm, k_out), refs = refs[:3], refs[3:]
    tables_vmem, refs = refs[:TABLES], refs[TABLES:]
    fxh, fxl, ixh, ixl, fyh, fyl, iyh, iyl, bzh, bzl, gather, spreader, eyz, ex = tables_vmem
    (
    vel, inc, tb, db, tf, df, s1, a2, w, hs, g0y, g0z, g1y, g1z,
    zsend, zout, zfrom, zpad, wpad, ssend, sout, sfrom, spad, qsend, qout, qfrom, qpad,
    tysend, tyfrom, sysend, syfrom, qysend, qyfrom, rims,
    su, sw, sh, fsend, frecv, bsend, brecv,
    load_sem, zs, zr, ys, yr, rs, rr, fs, fr, bs, br, store_sem,
        table_sem,
    ) = refs
    gz = lax.axis_index("gz")
    gy = lax.axis_index("gy")
    ynext, yprev = lax.rem(gy + 1, GY), lax.rem(gy + GY - 1, GY)
    znext, zprev = lax.rem(gz + 1, GZ), lax.rem(gz + GZ - 1, GZ)
    row = lax.broadcasted_iota(jnp.int32, (8, 128), 0)
    lane = lax.broadcasted_iota(jnp.int32, (8, 128), 1)
    slot = lax.rem(lax.shift_right_logical(lane + 2, 2), PACK)
    low_half = lax.rem(lane + 2, 4) < 2

    barrier = pltpu.get_barrier_semaphore()
    packs = NX // PACK

    def wrapped(k, count):
        return lax.select(k >= count, k - count, k)

    def each_peer(act):
        for kz in range(GZ):
            z = wrapped(gz + kz, GZ)

            def one(ky, carry):
                act(kz * GY + ky, z, wrapped(gy + ky, GY))
                return carry

            if kz == 0:
                for ky in range(1, 8):
                    one(ky, 0)
            lax.fori_loop(0 if kz else 8, GY, one, 0, unroll=8)

    def greet(k, z, y):
        pl.semaphore_signal(barrier, inc=1, device_id=(z, y), device_id_type=MESH)

    loads = [
        pltpu.make_async_copy(src, dst, load_sem.at[i])
        for i, (src, dst) in enumerate(
            [(t_hbm, tb), (d_hbm, db)]
            + [(u_hbm.at[pl.ds(c * NR, NR)], inc.at[pl.ds(PAD + c * NR, NR)]) for c in range(3)]
            + [(v_hbm.at[pl.ds(c * NR, NR)], vel.at[pl.ds(PAD + c * NR, NR)]) for c in range(3)]
        )
    ]
    fetches = [
        pltpu.make_async_copy(src, dst, table_sem.at[i]) for i, (src, dst) in enumerate(zip(tables_hbm, tables_vmem))
    ]
    for load in loads[:5]:
        load.start()
    each_peer(greet)

    def plane(ref, c, x):
        return ref[pl.ds(first(PAD + c * NR + x * 8), 8), :]

    def put(ref, c, x, value):
        ref[pl.ds(first(PAD + c * NR + x * 8), 8), :] = value

    def y_up(ref, c, x):
        return ref[pl.ds(PAD + 1 + c * NR + x * 8, 8), :]

    def y_down(ref, c, x):
        return ref[pl.ds(PAD - 1 + c * NR + x * 8, 8), :]

    def walk(ref, c, k):
        before = plane(ref, c, lax.rem(PACK * k + NX - 1, NX))
        here = plane(ref, c, PACK * k)
        for p in range(PACK):
            x = PACK * k + p + 1
            after = plane(ref, c, x if p < PACK - 1 else lax.rem(x, NX))
            yield before, here, after
            before, here = here, after

    def roll(value, shift, axis):
        return pltpu.roll(value, shift % value.shape[axis], axis)

    def pack_into(acc, value, p):
        return jnp.where(slot == p, roll(value, 4 * p, 1), acc)

    def unpacked(ref, f, k, p):
        return roll(ref[pl.ds(first(f * 64 + k * 8), 8), :], -4 * p, 1)

    def z_sides(value, outer):
        up = roll(jnp.where(lane == 0, outer, value), -1, 1)
        down = roll(jnp.where(lane == 127, outer, value), 1, 1)
        return up, down

    def halo_row(ref, k, x):
        return jnp.broadcast_to(ref[pl.ds(k * NX + x, 1), :], (8, 128))

    def spread(ref, base, k, r):
        return ref[pl.ds(PAD + base + 64 * k + r, 8, stride=8), :]

    def fold(packed, send, count):
        def one(m, carry):
            even = packed[pl.ds(first(m * 16), 8), :]
            odd = packed[pl.ds(first(m * 16 + 8), 8), :]
            at = pl.ds(first(m * 8), 8)
            send[0, at, :] = jnp.where(low_half, even, roll(odd, 2, 1))
            send[1, at, :] = jnp.where(low_half, roll(odd, -2, 1), even)
            return carry
        lax.fori_loop(0, count * 4, one, 0)

    def z_pair(send, got, sems, sem_at):
        return [
            pltpu.make_async_remote_copy(
                src_ref=send.at[side], dst_ref=got.at[side], send_sem=sems[0].at[sem_at + side],
                recv_sem=sems[1].at[sem_at + side], device_id=(to, gy), device_id_type=MESH)
            for side, to in ((0, znext), (1, zprev))
        ]

    def y_pair(send, got, sems, sem_at):
        return [
            pltpu.make_async_remote_copy(
                src_ref=send.at[side], dst_ref=got.at[side], send_sem=sems[0].at[sem_at + side],
                recv_sem=sems[1].at[sem_at + side], device_id=(gz, to), device_id_type=MESH)
            for side, to in ((0, ynext), (1, yprev))
        ]

    def combine(got, pad, count):
        def one(m, carry):
            at = pl.ds(first(m * 8), 8)
            below, above = got[0, at, :], got[1, at, :]
            pad[pl.ds(first(m * 16), 8), :] = jnp.where(low_half, below, above)
            pad[pl.ds(first(m * 16 + 8), 8), :] = jnp.where(low_half, roll(below, -2, 1), roll(above, 2, 1))
            return carry
        lax.fori_loop(0, count * 4, one, 0)

    loads[0].wait()
    loads[1].wait()

    def widen(k, carry):
        at = pl.ds(pl.multiple_of(k * 64, 64), 64)
        to = pl.ds(first(PAD + k * 64), 64)
        tf[to, :] = tb[at, :].astype(jnp.float32)
        df[to, :] = db[at, :].astype(jnp.float32)
        return carry

    lax.fori_loop(0, NR // 64, widen, 0)

    def state_rows(k, carry):
        at = pl.ds(first(8 * k), 8)
        also = pl.ds(first(NX + 8 * k), 8)
        tysend[0, at, :] = spread(tf, 0, k, 7)
        tysend[0, also, :] = spread(df, 0, k, 7)
        tysend[1, at, :] = spread(tf, 0, k, 0)
        tysend[1, also, :] = spread(df, 0, k, 0)
        return carry

    lax.fori_loop(0, NX // 8, state_rows, 0)
    for c in range(3):
        loads[2 + c].wait()
    for load in loads[5:] + fetches:
        load.start()
    sources = [(tf, 0), (df, 0), (inc, 0), (inc, 1), (inc, 2)]

    def inner_rows(n, carry):
        c, k = n // 32, lax.rem(n, 32)
        at = pl.ds(first(8 * k), 8)
        rims[0, c, 1, at, :] = spread(inc, c * NR, k, 7)
        rims[1, c, 1, at, :] = spread(inc, c * NR, k, 0)
        return carry

    def outer_rows(n, carry):
        c, k = n // 32, lax.rem(n, 32)
        at = pl.ds(first(8 * k), 8)
        rims[0, c, 0, at, :] = -(spread(inc, c * NR, k, 6) + 2.0 * spread(w, c * NR, k, 7))
        rims[1, c, 0, at, :] = -(spread(inc, c * NR, k, 1) + 2.0 * spread(w, c * NR, k, 0))
        return carry

    rim_copies = {
        (c, kind): [
            pltpu.make_async_remote_copy(
                src_ref=rims.at[side, c, kind], dst_ref=rim_hbm.at[side, c, kind],
                send_sem=rs.at[side * 6 + c * 2 + kind], recv_sem=rr.at[side * 6 + c * 2 + kind],
                device_id=(gz, to), device_id_type=MESH)
            for side, to in ((0, ynext), (1, yprev))
        ]
        for c in range(3) for kind in range(2)
    }

    def begin_rims(*which):
        for one in which:
            for copy in rim_copies[one]:
                copy.start()

    lax.fori_loop(0, 96, inner_rows, 0)

    def pack_inputs(k, carry):
        for f, (ref, c) in enumerate(sources):
            acc = jnp.zeros((8, 128), jnp.float32)
            for p in range(PACK):
                acc = pack_into(acc, plane(ref, c, PACK * k + p), p)
            zsend[pl.ds(first(f * 64 + k * 8), 8), :] = acc
        return carry

    lax.fori_loop(0, packs, pack_inputs, 0)
    fold(zsend, zout, 5)
    pl.semaphore_wait(barrier, GY * GZ - 1)
    state_copies = y_pair(tysend, tyfrom, (ys, yr), 0)
    edge_copies = z_pair(zout, zfrom, (zs, zr), 0)
    for copy in edge_copies + state_copies:
        copy.start()

    for copy in edge_copies:
        copy.wait_recv()
    combine(zfrom, zpad, 5)

    def edge_laplacian(n, carry):
        c, k = n // 8, lax.rem(n, 8)
        base = 128 + c * 64

        def tile(ref, m):
            return ref[pl.ds(first(base + m * 8), 8), :]

        here, own = tile(zpad, k), tile(zsend, k)
        before, after = tile(zpad, lax.rem(k + 7, 8)), tile(zpad, lax.rem(k + 1, 8))
        x_down = jnp.where(slot == 0, roll(before, 4, 1), roll(here, 4, 1))
        x_up = jnp.where(slot == PACK - 1, roll(after, -4, 1), roll(here, -4, 1))
        y_sum = jnp.where(row == 7, 0.0, roll(here, -1, 0)) + jnp.where(row == 0, 0.0, roll(here, 1, 0))
        z_sum = jnp.where(low_half, roll(here, 1, 1) + roll(own, -1, 1), roll(here, -1, 1) + roll(own, 1, 1))
        wpad[pl.ds(first(c * 64 + k * 8), 8), :] = 6.0 * here - (x_down + x_up) - y_sum - z_sum
        return carry

    lax.fori_loop(0, 24, edge_laplacian, 0)

    def y_sum_closed(ref, c, x, beyond):
        return jnp.where(row == 7, beyond, y_up(ref, c, x)) + jnp.where(row == 0, beyond, y_down(ref, c, x))

    def laplacian(n, carry):
        c, k = n // packs, lax.rem(n, packs)
        cells = walk(inc, c, k)
        for i in range(PACK // GROUP):
            sum_u = jnp.zeros((8, 128), jnp.float32)
            sum_w = jnp.zeros((8, 128), jnp.float32)
            for p in range(GROUP * i, GROUP * i + GROUP):
                x = PACK * k + p
                before, u, after = next(cells)
                up, down = z_sides(u, unpacked(zpad, 2 + c, k, p))
                lap = 6.0 * u - (before + after) - y_sum_closed(inc, c, x, 0.0) - (up + down)
                put(w, c, x, lap)
                sum_u = sum_u + u
                sum_w = sum_w + lap
            at = pl.ds(first(c * 512 + k * 64 + i * 8), 8)
            su[at, :] = sum_u
            sw[at, :] = sum_w
        return carry

    lax.fori_loop(0, packs, laplacian, 0)

    for copy in state_copies:
        copy.wait_recv()

    begin_rims((0, 1))

    def differences(ref, field, k, keep_y, keep_z):
        for p, (before, here, after) in enumerate(walk(ref, 0, k)):
            x = PACK * k + p
            z_up, z_down = z_sides(here, unpacked(zpad, field, k, p))
            up = jnp.where(row == 7, halo_row(tyfrom.at[1], field, x), y_up(ref, 0, x))
            down = jnp.where(row == 0, halo_row(tyfrom.at[0], field, x), y_down(ref, 0, x))
            dy, dz = up - down, z_up - z_down
            put(keep_y, 0, x, dy)
            put(keep_z, 0, x, dz)
            yield after - before, dy, dz

    def first_state(k, carry):
        acc = jnp.zeros((8, 128), jnp.float32)
        for p, (dx, dy, dz) in enumerate(differences(tf, 0, k, g0y, g0z)):
            x = PACK * k + p
            value = -0.25 * (plane(inc, 0, x) * dx + plane(inc, 1, x) * dy + plane(inc, 2, x) * dz)
            put(s1, 0, x, value)
            acc = pack_into(acc, value, p)
        ssend[pl.ds(first(k * 8), 8), :] = acc
        return carry

    lax.fori_loop(0, packs, first_state, 0)
    fold(ssend, sout, 1)

    def s1_rows(k, carry):
        at = pl.ds(first(8 * k), 8)
        sysend[0, at, :] = spread(s1, 0, k, 7)
        sysend[1, at, :] = spread(s1, 0, k, 0)
        return carry

    lax.fori_loop(0, NX // 8, s1_rows, 0)
    s1_copies = z_pair(sout, sfrom, (zs, zr), 2) + y_pair(sysend, syfrom, (ys, yr), 2)
    for copy in s1_copies:
        copy.start()


    def fine(n, carry):
        c, k = n // packs, lax.rem(n, packs)
        for p, (before, lap, after) in enumerate(walk(w, c, k)):
            x = PACK * k + p
            u = plane(inc, c, x)
            up, down = z_sides(lap, unpacked(wpad, c, k, p))
            twice = 6.0 * lap - (before + after) - y_sum_closed(w, c, x, -u) - (up + down)
            put(hs, c, x, (OMEGA * GAMMA) * u + (OMEGA * BETA) * twice)
        return carry

    lax.fori_loop(packs, 3 * packs, laplacian, 0)
    lax.fori_loop(0, packs, fine, 0)

    for c in range(3):
        loads[5 + c].wait()
    for copy in s1_copies:
        copy.wait_recv()
    begin_rims((1, 1), (2, 1))
    combine(sfrom, spad, 1)

    def second_state(k, carry):
        acc = jnp.zeros((8, 128), jnp.float32)
        both = zip(differences(df, 1, k, g1y, g1z), walk(s1, 0, k))
        for p, ((dx, dy, dz), (s_before, s, s_after)) in enumerate(both):
            x = PACK * k + p
            z_up, z_down = z_sides(s, unpacked(spad, 0, k, p))
            up = jnp.where(row == 7, halo_row(syfrom.at[1], 0, x), y_up(s1, 0, x))
            down = jnp.where(row == 0, halo_row(syfrom.at[0], 0, x), y_down(s1, 0, x))
            moved = 0.5 * (plane(inc, 0, x) * dx + plane(inc, 1, x) * dy + plane(inc, 2, x) * dz)
            speed = None
            for c, (after, before) in enumerate(((s_after, s_before), (up, down), (z_up, z_down))):
                speed = plane(vel, c, x)
                moved = moved + jnp.maximum(speed, 0.0) * (s - before) + jnp.minimum(speed, 0.0) * (after - s)
            value = 0.5 * moved - s
            put(a2, 0, x, value)
            sent = jnp.where(lane >= 64, jnp.minimum(speed, 0.0), jnp.maximum(speed, 0.0)) * value
            acc = pack_into(acc, sent, p)
        qsend[pl.ds(first(k * 8), 8), :] = acc
        return carry

    lax.fori_loop(0, packs, second_state, 0)
    fold(qsend, qout, 1)

    def flux_rows(k, carry):
        at = pl.ds(first(8 * k), 8)
        qysend[0, at, :] = jnp.minimum(spread(vel, NR, k, 7), 0.0) * spread(a2, 0, k, 7)
        qysend[1, at, :] = jnp.maximum(spread(vel, NR, k, 0), 0.0) * spread(a2, 0, k, 0)
        return carry

    lax.fori_loop(0, NX // 8, flux_rows, 0)
    flux_copies = z_pair(qout, qfrom, (zs, zr), 4) + y_pair(qysend, qyfrom, (ys, yr), 4)
    for copy in flux_copies:
        copy.start()
    lax.fori_loop(0, 96, outer_rows, 0)
    lax.fori_loop(packs, 3 * packs, fine, 0)
    for copy in flux_copies:
        copy.wait_recv()
    begin_rims((0, 0))
    combine(qfrom, qpad, 1)

    def adjoint(k, carry):
        sums = []
        fields = zip(walk(a2, 0, k), walk(vel, 0, k), walk(tf, 0, k), walk(df, 0, k))
        for p, (near_a, near_v, near_t, near_d) in enumerate(fields):
            x = PACK * k + p
            if p % GROUP == 0:
                sums = [jnp.zeros((8, 128), jnp.float32) for _ in range(3)]
            a = near_a[1]
            vy, vz = plane(vel, 1, x), plane(vel, 2, x)
            size = jnp.abs(near_v[1]) + jnp.abs(vy) + jnp.abs(vz)
            change = jnp.maximum(near_v[2], 0.0) * near_a[2]
            change = change - jnp.minimum(near_v[0], 0.0) * near_a[0] - size * a
            p_up = jnp.maximum(y_up(vel, 1, x), 0.0) * y_up(a2, 0, x)
            q_down = jnp.minimum(y_down(vel, 1, x), 0.0) * y_down(a2, 0, x)
            change = change + jnp.where(row == 7, halo_row(qyfrom.at[1], 0, x), p_up)
            change = change - jnp.where(row == 0, halo_row(qyfrom.at[0], 0, x), q_down)
            qz, pz = jnp.minimum(vz, 0.0) * a, jnp.maximum(vz, 0.0) * a
            outer = unpacked(qpad, 0, k, p)
            change = change + roll(jnp.where(lane == 0, outer, pz), -1, 1)
            change = change - roll(jnp.where(lane == 127, outer, qz), 1, 1)
            scaled = (0.25 * OMEGA) * (a + 0.5 * change)
            other = (0.25 * OMEGA) * a
            pairs = (
                (near_t[2] - near_t[0], near_d[2] - near_d[0]),
                (plane(g0y, 0, x), plane(g1y, 0, x)),
                (plane(g0z, 0, x), plane(g1z, 0, x)),
            )
            for c, (from_t, from_d) in enumerate(pairs):
                value = plane(hs, c, x) + scaled * from_t + other * from_d
                put(hs, c, x, value)
                sums[c] = sums[c] + value
            if p % GROUP == GROUP - 1:
                for c in range(3):
                    sh[pl.ds(first(c * 512 + k * 64 + p // GROUP * 8), 8), :] = sums[c]
        return carry

    lax.fori_loop(0, packs, adjoint, 0)
    store = pltpu.make_async_copy(hs.at[pl.ds(PAD, 3 * NR)], h_hbm, store_sem)
    store.start()

    def rows_of(ref, c, r):
        return ref[pl.ds(c * 512 + r, CX, stride=8), :]

    for fetch in fetches:
        fetch.wait()

    def contribute():
        parts = []
        for c in range(3):
            scale = OMEGA * BETA
            parts.append(scale * (rows_of(su, c, 0) - rows_of(su, c, 1) - 2.0 * rows_of(sw, c, 0)))
            for half in (0, 4):
                parts.append(
                    (rows_of(sh, c, half) + rows_of(sh, c, half + 1))
                    + (rows_of(sh, c, half + 2) + rows_of(sh, c, half + 3)))
            parts.append(scale * (rows_of(su, c, 7) - rows_of(su, c, 6) - 2.0 * rows_of(sw, c, 7)))
        for c in range(3):
            lines = mm((fxh[...], fxl[...]), jnp.concatenate(parts[4 * c:4 * c + 4], axis=1))
            lines = mm(lines, (gather[...], None))
            for h in range(2):
                block = lines[h * GY:(h + 1) * GY]
                if c < 2:
                    fsend[h * GY:(h + 1) * GY, c, :] = block
                else:
                    fsend[(2 + h) * GY:(3 + h) * GY, 0, :] = block
                    fsend[(2 + h) * GY:(3 + h) * GY, 1, :] = block

    contribute()
    me = gz * GY + gy

    def exchange(send, got, ssem, rsem):
        def begin(k, z, y):
            pltpu.make_async_remote_copy(
                src_ref=send.at[z * GY + y], dst_ref=got.at[me], send_sem=ssem, recv_sem=rsem,
                device_id=(z, y), device_id_type=MESH).start()

        each_peer(begin)
        pltpu.make_async_copy(send.at[me], got.at[me], rsem).start()

        def finish():
            pltpu.make_async_copy(got, got, rsem).wait()

        def done():
            others = pl.ds(0, GY * GZ - 1)
            pltpu.make_async_copy(send.at[others], send.at[others], ssem).wait()

        return finish, done

    arrive, sent_forward = exchange(fsend, frecv, fs, fr)
    begin_rims((1, 0), (2, 0))
    total = eyz[...] + ex[pl.ds(2 * gy + lax.rem(gz, 2), 1), :]
    factor = (1.0 / (GAMMA + COARSE_BETA * total * total) - OMEGA) * (1.0 / (OMEGA * CX * CY * CZ))
    arrive()
    lane64 = lax.broadcasted_iota(jnp.int32, (CY, 128), 1) // 32
    lane32 = lax.broadcasted_iota(jnp.int32, (GY, 128), 1) // 32
    def solve():
        solved = []
        for s in range(2):
            whole = jnp.zeros((CY, 128), jnp.float32)
            for zb in range(GZ):
                lines = mm((fyh[...], fyl[...]), frecv[zb * GY:(zb + 1) * GY, s, :])
                merged = jnp.zeros((CY, 128), jnp.float32)
                for j in range(4):
                    moved = roll(lines[j * CY:(j + 1) * CY], 32 * (zb - j), 1)
                    merged = merged + moved
                whole = jnp.where(lane64 == zb, merged, whole)
            table_z = (bzh[...], bzl[...])
            modes = mm(whole, table_z) * factor
            solved.append(mm((iyh[...], iyl[...]), mm(modes, table_z)))
        for zb in range(GZ):
            block = jnp.zeros((GY, 128), jnp.float32)
            for s in range(2):
                for half in range(2):
                    part = roll(solved[s][half * GY:(half + 1) * GY], 32 * (2 * s + half - zb), 1)
                    block = jnp.where(lane32 == 2 * s + half, part, block)
            bsend[zb * GY:(zb + 1) * GY, 0, :] = block

    solve()
    arrive, sent_back = exchange(bsend, brecv, bs, br)
    arrive()
    def bring_back():
        for k in range(2):
            modes = brecv[2 * k * GY:(2 * k + 2) * GY, 0, :]
            lines = mm((ixh[...], ixl[...]), modes)
            count = 4 if k == 0 else 2
            wide = mm(lines, (spreader[:, :count * 128], None))
            for n in range(count):
                k_out[pl.ds((4 * k + n) * CX, CX), :] = wide[:, n * 128:(n + 1) * 128]

    bring_back()
    sent_forward()
    sent_back()
    for copy in edge_copies + state_copies + s1_copies + flux_copies:
        copy.wait_send()
    for pair in rim_copies.values():
        for copy in pair:
            copy.wait()
    store.wait()


def finish(h_ref, rim_ref, k_ref, out_ref):
    row = lax.broadcasted_iota(jnp.int32, (8, 128), 0)

    def one(c, carry):
        for p in range(h_ref.shape[1]):
            def wide(ref):
                return jnp.broadcast_to(ref[pl.ds(p, 1), :], (8, 128))

            rim = jnp.where(
                row < 4, *(jnp.broadcast_to(k_ref[2 * c + half, pl.ds(p // 4, 1), :], (8, 128)) for half in (0, 1)))
            late = jnp.zeros((8, 128), jnp.float32)
            for at, side, kind in ((0, 0, 0), (1, 0, 1), (6, 1, 1), (7, 1, 0)):
                late = jnp.where(row == at, wide(rim_ref.at[side, c, kind]), late)
            out_ref[c, p] = h_ref[c, p] + (rim + (OMEGA * BETA) * late)
        return carry

    lax.fori_loop(0, 3, one, 0)


def per_device(velocity, increment, template, deformed):
    consts = [jnp.asarray(t) for t in tables()]
    f32 = jnp.float32
    vm = lambda *shape: pltpu.VMEM(shape, f32)
    dma = pltpu.SemaphoreType.DMA
    hessian, rims, coarse = pl.pallas_call(
        action,
        out_shape=(
            jax.ShapeDtypeStruct((3 * NR, 128), f32),
            jax.ShapeDtypeStruct((2, 3, 2, NX, 128), f32),
            jax.ShapeDtypeStruct((6 * CX, 128), f32),
        ),
        in_specs=[pl.BlockSpec(memory_space=pl.ANY)] * (4 + len(consts)),
        out_specs=(
            pl.BlockSpec(memory_space=pl.ANY),
            pl.BlockSpec(memory_space=pl.ANY),
            pl.BlockSpec(memory_space=pltpu.VMEM),
        ),
        scratch_shapes=[
            *[pltpu.VMEM(t.shape, t.dtype) for t in consts],
            vm(3 * NR + 2 * PAD, 128), vm(3 * NR + 2 * PAD, 128),
            pltpu.VMEM((NR, 128), jnp.bfloat16), pltpu.VMEM((NR, 128), jnp.bfloat16),
            *[vm(NR + 2 * PAD, 128)] * 4, *[vm(3 * NR + 2 * PAD, 128)] * 2, *[vm(NR + 2 * PAD, 128)] * 4,
            vm(320, 128), vm(2, 160, 128), vm(2, 160, 128), vm(320, 128), vm(192, 128),
            *[vm(64, 128), vm(2, 32, 128), vm(2, 32, 128), vm(64, 128)] * 2,
            vm(2, 2 * NX, 128), vm(2, 2 * NX, 128), vm(2, NX, 128), vm(2, NX, 128), vm(2, NX, 128), vm(2, NX, 128),
            vm(2, 3, 2, NX, 128),
            vm(3 * 512, 128), vm(3 * 512, 128), vm(3 * 512, 128),
            vm(GZ * GY, 2, 128), vm(GZ * GY, 2, 128), vm(GZ * GY, 1, 128), vm(GZ * GY, 1, 128),
            dma((8,)), dma((6,)), dma((6,)), dma((6,)), dma((6,)), dma((12,)), dma((12,)),
            dma, dma, dma, dma, dma, dma((TABLES,)),
        ],
        compiler_params=pltpu.CompilerParams(
            collective_id=1, has_side_effects=True, vmem_limit_bytes=56 * 1024 * 1024),
        name="action",
    )(
        velocity.reshape(3 * NR, 128), increment.reshape(3 * NR, 128),
        template.reshape(NR, 128), deformed.reshape(NR, 128), *consts,
    )
    step = 32
    return pl.pallas_call(
        finish,
        grid=(NX // step,),
        out_shape=jax.ShapeDtypeStruct((3, NX, 8, 128), f32),
        in_specs=[
            pl.BlockSpec((3, step, 8, 128), lambda i: (0, i, 0, 0)),
            pl.BlockSpec((2, 3, 2, step, 128), lambda i: (0, 0, 0, i, 0)),
            pl.BlockSpec((6, step // 4, 128), lambda i: (0, i, 0)),
        ],
        out_specs=pl.BlockSpec((3, step, 8, 128), lambda i: (0, i, 0, 0)),
        name="finish",
    )(hessian.reshape(3, NX, 8, 128), rims, coarse.reshape(6, CX, 128))


def solution(mesh):
    placed = (
        P(None, None, "gy", "gz"),
        P(None, None, "gy", "gz"),
        P(None, "gy", "gz"),
        P(None, "gy", "gz"),
    )
    return jax.shard_map(
        per_device, mesh=mesh, in_specs=placed, out_specs=P(None, None, "gy", "gz"), check_vma=False
    )
```

time: 133 us -> 77.5 us (0.58)
  Pallas kernels: 133 us -> 77.3 us
    pallas_call x1, Pallas kernels: 126 us -> 70.4 us  [per_device(): pl.pallas_call(action, out_shape=(jax.ShapeDtypeStruct((3 * NR, 128), f32...]
where the time goes in v1:
time: 77.5 us; the launch traced here: 77.3 us
  Pallas kernels  77.3 us (100%)
    pallas_call x1, Pallas kernels, per_device(): pl.pallas_call(action, out_shape=(jax.ShapeDtypeStruct((3 * NR, 128), f32...  70.4 us
    pallas_call x1, Pallas kernels, per_device(): pl.pallas_call(finish, grid=(NX // step,), out_shape=jax.ShapeDtypeStruct...  6.82 us

profile of v1, /device:TPU:1, one launch (start us, length us, event | category | flops | bytes accessed | tf_op | source)
XLA Modules:
  0.0 77.3 jit_solution(10681847118782683837)
XLA Ops:
  0.0 70.4 %action.1 = (f32[6144,128]{1,0:T(8,128)}, f32[2,3,2,256,128]{4,3,2,1,0:T(8,128)}, f32[384,128]{1,0:T(8,128)}) custom-call(f32[6144,128]{1,0:T(8,128)} %bitcast.6, f32[6144,128]{1,0:T(8,128)} %bitcast.7, bf16[2048,128]{1,0:T(8,128)(2,1)} %bitcast.9, bf16[2048,128]{1,0:T(8,128)(2,1)} %bitcast.10, bf16[64,64]{1,0:T(8,128)(2,1)} %constant.24.clone.refs_0_.refs_6_, ...), custom_call_target="tpu_custom_call" | custom-call | tf_op jit(solution)/shard_map/action/pallas_call | solution.py:606
  70.4 6.8 %finish.1 = f32[3,256,8,128]{3,2,1,0:T(8,128)} custom-call(f32[3,256,8,128]{3,2,1,0:T(8,128)} %bitcast.8, f32[2,3,2,256,128]{4,3,2,1,0:T(8,128)} %get-tuple-element.9.rim_ref, f32[6,64,128]{2,1,0:T(8,128)} %bitcast.11), custom_call_target="tpu_custom_call" | custom-call | tf_op jit(solution)/shard_map/finish/pallas_call | solution.py:641

commit v2 on v1

--- a/solution.py
+++ b/solution.py
@@ -83,15 +83,15 @@
     *refs,
 ):
     tables_hbm, refs = refs[:TABLES], refs[TABLES:]
-    (h_hbm, rim_hbm, k_out), refs = refs[:3], refs[3:]
+    (hs, rim_in, k_out), refs = refs[:3], refs[3:]
     tables_vmem, refs = refs[:TABLES], refs[TABLES:]
     fxh, fxl, ixh, ixl, fyh, fyl, iyh, iyl, bzh, bzl, gather, spreader, eyz, ex = tables_vmem
     (
-    vel, inc, tb, db, tf, df, s1, a2, w, hs, g0y, g0z, g1y, g1z,
+    vel, inc, tb, db, tf, df, s1, a2, w, g0y, g0z, g1y, g1z,
     zsend, zout, zfrom, zpad, wpad, ssend, sout, sfrom, spad, qsend, qout, qfrom, qpad,
     tysend, tyfrom, sysend, syfrom, qysend, qyfrom, rims,
     su, sw, sh, fsend, frecv, bsend, brecv,
-    load_sem, zs, zr, ys, yr, rs, rr, fs, fr, bs, br, store_sem,
+    load_sem, zs, zr, ys, yr, rs, rr, fs, fr, bs, br,
         table_sem,
     ) = refs
     gz = lax.axis_index("gz")
@@ -261,7 +261,7 @@
     rim_copies = {
         (c, kind): [
             pltpu.make_async_remote_copy(
-                src_ref=rims.at[side, c, kind], dst_ref=rim_hbm.at[side, c, kind],
+                src_ref=rims.at[side, c, kind], dst_ref=rim_in.at[side, c, kind],
                 send_sem=rs.at[side * 6 + c * 2 + kind], recv_sem=rr.at[side * 6 + c * 2 + kind],
                 device_id=(gz, to), device_id_type=MESH)
             for side, to in ((0, ynext), (1, yprev))
@@ -476,8 +476,6 @@
         return carry
 
     lax.fori_loop(0, packs, adjoint, 0)
-    store = pltpu.make_async_copy(hs.at[pl.ds(PAD, 3 * NR)], h_hbm, store_sem)
-    store.start()
 
     def rows_of(ref, c, r):
         return ref[pl.ds(c * 512 + r, CX, stride=8), :]
@@ -576,26 +574,43 @@
     for pair in rim_copies.values():
         for copy in pair:
             copy.wait()
-    store.wait()
-
-
-def finish(h_ref, rim_ref, k_ref, out_ref):
+
+
+def finish(h_ref, rim_ref, k_ref, out_hbm, out, sems):
     row = lax.broadcasted_iota(jnp.int32, (8, 128), 0)
-
-    def one(c, carry):
-        for p in range(h_ref.shape[1]):
+    planes = 64
+
+    def copy(n):
+        rows = pl.ds(pl.multiple_of(n * planes * 8, 8), planes * 8)
+        return pltpu.make_async_copy(out.at[rows], out_hbm.at[rows], sems.at[n])
+
+    def one(n, carry):
+        c, part = n // (NX // planes), lax.rem(n, NX // planes)
+        for p in range(planes):
+            x = part * planes + p
+
             def wide(ref):
-                return jnp.broadcast_to(ref[pl.ds(p, 1), :], (8, 128))
+                return jnp.broadcast_to(ref[pl.ds(x, 1), :], (8, 128))
 
             rim = jnp.where(
-                row < 4, *(jnp.broadcast_to(k_ref[2 * c + half, pl.ds(p // 4, 1), :], (8, 128)) for half in (0, 1)))
+                row < 4,
+                *(jnp.broadcast_to(k_ref[pl.ds((2 * c + half) * CX + part * (planes // 4) + p // 4, 1), :], (8, 128))
+                  for half in (0, 1)))
             late = jnp.zeros((8, 128), jnp.float32)
             for at, side, kind in ((0, 0, 0), (1, 0, 1), (6, 1, 1), (7, 1, 0)):
                 late = jnp.where(row == at, wide(rim_ref.at[side, c, kind]), late)
-            out_ref[c, p] = h_ref[c, p] + (rim + (OMEGA * BETA) * late)
-        return carry
-
-    lax.fori_loop(0, 3, one, 0)
+            at = first((n * planes + p) * 8)
+            out[pl.ds(at, 8), :] = h_ref[pl.ds(PAD + at, 8), :] + (rim + (OMEGA * BETA) * late)
+        copy(n).start()
+        return carry
+
+    lax.fori_loop(0, 3 * NX // planes, one, 0)
+
+    def drain(n, carry):
+        copy(n).wait()
+        return carry
+
+    lax.fori_loop(0, 3 * NX // planes, drain, 0)
 
 
 def per_device(velocity, increment, template, deformed):
@@ -606,21 +621,17 @@
     hessian, rims, coarse = pl.pallas_call(
         action,
         out_shape=(
-            jax.ShapeDtypeStruct((3 * NR, 128), f32),
-            jax.ShapeDtypeStruct((2, 3, 2, NX, 128), f32),
-            jax.ShapeDtypeStruct((6 * CX, 128), f32),
+            vm(3 * NR + 2 * PAD, 128),
+            vm(2, 3, 2, NX, 128),
+            vm(6 * CX, 128),
         ),
-        in_specs=[pl.BlockSpec(memory_space=pl.ANY)] * (4 + len(consts)),
-        out_specs=(
-            pl.BlockSpec(memory_space=pl.ANY),
-            pl.BlockSpec(memory_space=pl.ANY),
-            pl.BlockSpec(memory_space=pltpu.VMEM),
-        ),
+        in_specs=[pl.BlockSpec(memory_space=pltpu.HBM)] * (4 + len(consts)),
+        out_specs=[pl.BlockSpec(memory_space=pltpu.VMEM)] * 3,
         scratch_shapes=[
             *[pltpu.VMEM(t.shape, t.dtype) for t in consts],
             vm(3 * NR + 2 * PAD, 128), vm(3 * NR + 2 * PAD, 128),
             pltpu.VMEM((NR, 128), jnp.bfloat16), pltpu.VMEM((NR, 128), jnp.bfloat16),
-            *[vm(NR + 2 * PAD, 128)] * 4, *[vm(3 * NR + 2 * PAD, 128)] * 2, *[vm(NR + 2 * PAD, 128)] * 4,
+            *[vm(NR + 2 * PAD, 128)] * 4, vm(3 * NR + 2 * PAD, 128), *[vm(NR + 2 * PAD, 128)] * 4,
             vm(320, 128), vm(2, 160, 128), vm(2, 160, 128), vm(320, 128), vm(192, 128),
             *[vm(64, 128), vm(2, 32, 128), vm(2, 32, 128), vm(64, 128)] * 2,
             vm(2, 2 * NX, 128), vm(2, 2 * NX, 128), vm(2, NX, 128), vm(2, NX, 128), vm(2, NX, 128), vm(2, NX, 128),
@@ -628,28 +639,26 @@
             vm(3 * 512, 128), vm(3 * 512, 128), vm(3 * 512, 128),
             vm(GZ * GY, 2, 128), vm(GZ * GY, 2, 128), vm(GZ * GY, 1, 128), vm(GZ * GY, 1, 128),
             dma((8,)), dma((6,)), dma((6,)), dma((6,)), dma((6,)), dma((12,)), dma((12,)),
-            dma, dma, dma, dma, dma, dma((TABLES,)),
+            dma, dma, dma, dma, dma((TABLES,)),
         ],
         compiler_params=pltpu.CompilerParams(
-            collective_id=1, has_side_effects=True, vmem_limit_bytes=56 * 1024 * 1024),
+            collective_id=1, has_side_effects=True, vmem_limit_bytes=40 * 1024 * 1024),
         name="action",
     )(
-        velocity.reshape(3 * NR, 128), increment.reshape(3 * NR, 128),
-        template.reshape(NR, 128), deformed.reshape(NR, 128), *consts,
+        *(pltpu.with_memory_space_constraint(x, pltpu.HBM) for x in (
+            velocity.reshape(3 * NR, 128), increment.reshape(3 * NR, 128),
+            template.reshape(NR, 128), deformed.reshape(NR, 128), *consts)),
     )
-    step = 32
-    return pl.pallas_call(
+    result = pl.pallas_call(
         finish,
-        grid=(NX // step,),
-        out_shape=jax.ShapeDtypeStruct((3, NX, 8, 128), f32),
-        in_specs=[
-            pl.BlockSpec((3, step, 8, 128), lambda i: (0, i, 0, 0)),
-            pl.BlockSpec((2, 3, 2, step, 128), lambda i: (0, 0, 0, i, 0)),
-            pl.BlockSpec((6, step // 4, 128), lambda i: (0, i, 0)),
-        ],
-        out_specs=pl.BlockSpec((3, step, 8, 128), lambda i: (0, i, 0, 0)),
+        out_shape=jax.ShapeDtypeStruct((3 * NR, 128), f32),
+        in_specs=[pl.BlockSpec(memory_space=pltpu.VMEM)] * 3,
+        out_specs=pl.BlockSpec(memory_space=pltpu.HBM),
+        scratch_shapes=[vm(3 * NR, 128), dma((12,))],
+        compiler_params=pltpu.CompilerParams(vmem_limit_bytes=16 * 1024 * 1024),
         name="finish",
-    )(hessian.reshape(3, NX, 8, 128), rims, coarse.reshape(6, CX, 128))
+    )(*(pltpu.with_memory_space_constraint(x, pltpu.VMEM) for x in (hessian, rims, coarse)))
+    return result.reshape(3, NX, 8, 128)
 
 
 def solution(mesh):

time: 77.5 us -> 71.7 us (0.925)
  Pallas kernels: 77.3 us -> 71.6 us
    pallas_call x2, Pallas kernels: 77.3 us -> 71.6 us  [the longest x1 69.6 us: per_device(): pl.pallas_call(action, out_shape=(vm(3 * NR + 2 * PAD, 128), vm(2, 3, 2,...]
where the time goes in v2:
time: 71.7 us; the launch traced here: 71.6 us
  Pallas kernels  71.6 us (100%)
    pallas_call x1, Pallas kernels, per_device(): pl.pallas_call(action, out_shape=(vm(3 * NR + 2 * PAD, 128), vm(2, 3, 2,...  69.6 us
    pallas_call x1, Pallas kernels, per_device(): pl.pallas_call(finish, out_shape=jax.ShapeDtypeStruct((3 * NR, 128), f32)...  2.01 us

profile of v2, /device:TPU:1, one launch (start us, length us, event | category | flops | bytes accessed | tf_op | source)
XLA Modules:
  0.0 71.6 jit_solution(9078108507334926366)
XLA Ops:
  0.0 69.6 %action.1 = (f32[6160,128]{1,0:T(8,128)S(1)}, f32[2,3,2,256,128]{4,3,2,1,0:T(8,128)S(1)}, f32[384,128]{1,0:T(8,128)S(1)}) custom-call(f32[6144,128]{1,0:T(8,128)} %bitcast.5, f32[6144,128]{1,0:T(8,128)} %bitcast.6, bf16[2048,128]{1,0:T(8,128)(2,1)} %bitcast.7, bf16[2048,128]{1,0:T(8,128)(2,1)} %bitcast.8, bf16[64,64]{1,0:T(8,128)(2,1)} %constant.24.clone.refs_0_.refs_6_, ...), custom_call_target="tpu_custom_call" | custom-call | tf_op jit(solution)/shard_map/action/pallas_call | solution.py:621
  69.6 2.0 %finish.1 = f32[6144,128]{1,0:T(8,128)} custom-call(f32[6160,128]{1,0:T(8,128)S(1)} %get-tuple-element.8.h_ref, f32[2,3,2,256,128]{4,3,2,1,0:T(8,128)S(1)} %get-tuple-element.9.rim_ref, f32[384,128]{1,0:T(8,128)S(1)} %get-tuple-element.10.k_ref), custom_call_target="tpu_custom_call" | custom-call | tf_op jit(solution)/shard_map/finish/pallas_call | solution.py:652

commit v3 on v2

--- a/solution.py
+++ b/solution.py
@@ -110,7 +110,7 @@
         return lax.select(k >= count, k - count, k)
 
     def each_peer(act):
-        for kz in range(GZ):
+        for kz in (2, 3, 1, 0):
             z = wrapped(gz + kz, GZ)
 
             def one(ky, carry):

time: 71.7 us -> 72.1 us (level)
  no operation moved by 1% of the time
where the time goes in v3:
time: 72.1 us; the launch traced here: 72 us
  Pallas kernels  72 us (100%)
    pallas_call x1, Pallas kernels, per_device(): pl.pallas_call(action, out_shape=(vm(3 * NR + 2 * PAD, 128), vm(2, 3, 2,...  70 us
    pallas_call x1, Pallas kernels, per_device(): pl.pallas_call(finish, out_shape=jax.ShapeDtypeStruct((3 * NR, 128), f32)...  2.01 us

profile of v3, /device:TPU:1, one launch (start us, length us, event | category | flops | bytes accessed | tf_op | source)
XLA Modules:
  0.0 72.0 jit_solution(18257912502928720569)
XLA Ops:
  0.0 70.0 %action.1 = (f32[6160,128]{1,0:T(8,128)S(1)}, f32[2,3,2,256,128]{4,3,2,1,0:T(8,128)S(1)}, f32[384,128]{1,0:T(8,128)S(1)}) custom-call(f32[6144,128]{1,0:T(8,128)} %bitcast.5, f32[6144,128]{1,0:T(8,128)} %bitcast.6, bf16[2048,128]{1,0:T(8,128)(2,1)} %bitcast.7, bf16[2048,128]{1,0:T(8,128)(2,1)} %bitcast.8, bf16[64,64]{1,0:T(8,128)(2,1)} %constant.24.clone.refs_0_.refs_6_, ...), custom_call_target="tpu_custom_call" | custom-call | tf_op jit(solution)/shard_map/action/pallas_call | solution.py:621
  70.0 2.0 %finish.1 = f32[6144,128]{1,0:T(8,128)} custom-call(f32[6160,128]{1,0:T(8,128)S(1)} %get-tuple-element.8.h_ref, f32[2,3,2,256,128]{4,3,2,1,0:T(8,128)S(1)} %get-tuple-element.9.rim_ref, f32[384,128]{1,0:T(8,128)S(1)} %get-tuple-element.10.k_ref), custom_call_target="tpu_custom_call" | custom-call | tf_op jit(solution)/shard_map/finish/pallas_call | solution.py:652
